TPU v7x, 32 devices: a whole 2x2x4 slice. The times are simulated.
32 devices in a mesh: pages: 2 (over y), tile: 4 (over z), mp: 2 (over x), batch: 2 (over core).
Axes of the slice: x: 2, y: 2, z: 4, core: 2. Of those that a mesh axis runs over, the one named last changes fastest.
Arguments:
- page_cells: bfloat16 [4, 48, 24, 1024], P(('pages', 'batch'), 'tile'), parts along dimension 0, may hold values from -40 to 40
- text_states: bfloat16 [4, 1024, 1024], P(('pages', 'batch'), 'tile'), parts along dimension 0, may hold values from -40 to 40
- enc_query: bfloat16 [1024, 1024], P('batch', 'mp'), may hold values from -2.5 to 2.5
- enc_keyval: bfloat16 [1024, 2, 1024], P('batch', None, 'mp'), may hold values from -0.1875 to 0.1875
- enc_proj: bfloat16 [1024, 1024], P('mp', 'batch'), may hold values from -0.1875 to 0.1875
- dec_query: bfloat16 [1024, 1024], P('batch', 'mp'), may hold values from -2.5 to 2.5
- dec_keyval: bfloat16 [1024, 2, 1024], P('batch', None, 'mp'), may hold values from -0.1875 to 0.1875
- dec_out: bfloat16 [1024, 1024], P('mp', 'batch'), may hold values from -0.1875 to 0.1875
Outputs:
- encoded: bfloat16 [4, 48, 24, 1024], P(('pages', 'batch'), 'tile'), parts along dimension 0
- decoded: bfloat16 [4, 1024, 1024], P(('pages', 'batch'), ('tile', 'mp')), parts along dimension 0
There are 2 independent parts, one for each index of `pages`. A program takes and returns all parts, laid end to end along the dimension named above; an argument that names none is the same for every part. Nothing has to cross between parts.
All inputs are finite; a program needn't handle non-finite values.
Results may differ from a plain program's by a relative error of at most 0.012.
Values may be sent and summed in bfloat16 or wider, within the bound.
No kernel may reach another device: no remote copies, remote signals or barrier semaphores. Data moves between devices by JAX's collectives and lax.ppermute only.
A program may use at most 64 MiB of HBM per device.

v0:
```python
import math
import jax
import jax.numpy as jnp
from jax import lax
from jax.sharding import PartitionSpec as P

HEAD_ENC = 32
HEAD_DEC = 64


def from_behind(value, axis, by):
    devices = lax.axis_size(axis)
    return lax.ppermute(value, axis, [(i, (i + by) % devices) for i in range(devices)])


def layer_norm(values):
    center = values - jnp.mean(values, axis=-1, keepdims=True)
    variance = jnp.mean(center * center, axis=-1, keepdims=True)
    return center / jnp.sqrt(variance + 1e-05)


def regions(length, window, offset):
    index_row = jnp.arange(length, dtype=jnp.int32)
    return jnp.where(
        index_row < length - window, 0, jnp.where(index_row < length - offset, 1, 2)
    ).astype(jnp.int32)


def body(page_cells, text_states, enc_query, enc_keyval, enc_proj, dec_query, dec_keyval, dec_out):
    wq_enc, wkv_enc, wproj_enc, wq_dec, wkv_dec, wout_dec = (
        lax.all_gather(enc_query, "batch", axis=0, tiled=True),
        lax.all_gather(enc_keyval, "batch", axis=0, tiled=True),
        lax.all_gather(enc_proj, "batch", axis=1, tiled=True),
        lax.all_gather(dec_query, "batch", axis=0, tiled=True),
        lax.all_gather(dec_keyval, "batch", axis=0, tiled=True),
        lax.all_gather(dec_out, "batch", axis=1, tiled=True),
    )
    pages_here, window, columns, width = page_cells.shape
    offset = window // 2
    own_rows = window * columns
    hq_enc = wq_enc.shape[1]
    heads_enc = hq_enc // HEAD_ENC
    joined = jnp.concatenate([wq_enc, wkv_enc.reshape(width, 2 * hq_enc)], axis=1)
    rows_below = from_behind(page_cells[:, :offset], "tile", -1)
    normed = layer_norm(
        jnp.concatenate([page_cells[:, offset:], rows_below], axis=1).astype(jnp.float32)
    ).astype(jnp.bfloat16)
    projected = jnp.einsum(
        "prcd,de->prce", normed, joined, preferred_element_type=jnp.float32
    ).astype(jnp.bfloat16)
    projected = jnp.roll(projected, -offset, axis=2)
    per_row = columns // window
    shaped = projected.reshape(pages_here, window, per_row, window, 3, heads_enc, HEAD_ENC)
    shaped = jnp.swapaxes(shaped, 1, 2).reshape(
        pages_here, per_row, window * window, 3, heads_enc, HEAD_ENC
    )
    win_q = shaped[:, :, :, 0]
    win_k = shaped[:, :, :, 1]
    win_v = shaped[:, :, :, 2]
    is_last = lax.axis_index("tile") == lax.axis_size("tile") - 1
    local_rows = jnp.arange(window, dtype=jnp.int32)
    row_region = jnp.where(is_last, jnp.where(local_rows < window - offset, 1, 2), 0).astype(
        jnp.int32
    )
    labels = row_region[:, None] * 3 + regions(columns, window, offset)[None, :]
    labels = jnp.swapaxes(labels.reshape(window, per_row, window), 0, 1).reshape(
        per_row, window * window
    )
    allowed = labels[:, :, None] == labels[:, None, :]
    win_scores = jnp.einsum(
        "pnqhd,pnkhd->pnhqk", win_q, win_k, preferred_element_type=jnp.float32
    ) / math.sqrt(HEAD_ENC)
    win_scores = jnp.where(allowed[None, :, None], win_scores, -jnp.inf)
    top = jnp.max(win_scores, axis=-1, keepdims=True)
    expd = jnp.exp(win_scores - top)
    win_weights = (expd / jnp.sum(expd, axis=-1, keepdims=True)).astype(jnp.bfloat16)
    win_out = jnp.einsum(
        "pnhqk,pnkhd->pnqhd", win_weights, win_v, preferred_element_type=jnp.float32
    ).astype(jnp.bfloat16)
    win_out = win_out.reshape(pages_here, per_row, window, window, hq_enc)
    win_out = jnp.swapaxes(win_out, 1, 2).reshape(pages_here, window, columns, hq_enc)
    win_out = jnp.roll(win_out, offset, axis=2)
    rows_above = from_behind(win_out[:, window - offset :], "tile", 1)
    unrolled = jnp.concatenate([rows_above, win_out[:, : window - offset]], axis=1)
    partial_proj = jnp.einsum(
        "prce,ed->prcd", unrolled, wproj_enc, preferred_element_type=jnp.float32
    )
    summed = lax.psum(partial_proj.astype(jnp.bfloat16), "mp").astype(jnp.float32)
    encoded = (page_cells.astype(jnp.float32) + summed).astype(jnp.bfloat16)
    hq_dec = wq_dec.shape[1]
    heads_dec = hq_dec // HEAD_DEC
    page_normed = (
        layer_norm(encoded.astype(jnp.float32))
        .astype(jnp.bfloat16)
        .reshape(pages_here, own_rows, width)
    )
    page_kv = jnp.einsum(
        "pnd,de->pne",
        page_normed,
        wkv_dec.reshape(width, 2 * hq_dec),
        preferred_element_type=jnp.float32,
    ).astype(jnp.bfloat16)
    text_normed = layer_norm(text_states.astype(jnp.float32)).astype(jnp.bfloat16)
    queries = jnp.einsum(
        "ptd,de->pte", text_normed, wq_dec, preferred_element_type=jnp.float32
    ).astype(jnp.bfloat16)
    text_len = text_states.shape[1]
    query_heads = queries.reshape(pages_here, text_len, heads_dec, HEAD_DEC)
    start_state = (
        jnp.full((pages_here, heads_dec, text_len), -jnp.inf, jnp.float32),
        jnp.zeros((pages_here, heads_dec, text_len), jnp.float32),
        jnp.zeros((pages_here, heads_dec, text_len, HEAD_DEC), jnp.float32),
    )
    carried = start_state
    shard_rows = lax.all_gather(page_kv, "tile", axis=1, tiled=True)
    count = shard_rows.shape[1] // own_rows
    grouped = max(
        (
            factor
            for factor in range(1, count + 1)
            if count % factor == 0 and factor * own_rows <= 2048
        )
    )
    blocks = jnp.moveaxis(
        shard_rows.reshape(pages_here, count // grouped, grouped * own_rows, 2 * hq_dec), 1, 0
    )

    def advance(running, block_kv):
        maxima, totals, accum = running
        span = block_kv.shape[1]
        block_keys = block_kv[..., :hq_dec].reshape(pages_here, span, heads_dec, HEAD_DEC)
        block_vals = block_kv[..., hq_dec:].reshape(pages_here, span, heads_dec, HEAD_DEC)
        cross_scores = jnp.einsum(
            "pqhd,pkhd->phqk", query_heads, block_keys, preferred_element_type=jnp.float32
        ) / math.sqrt(HEAD_DEC)
        newest = jnp.maximum(maxima, jnp.max(cross_scores, axis=-1))
        rescale = jnp.exp(maxima - newest)
        expo = jnp.exp(cross_scores - newest[..., None])
        totals = totals * rescale + jnp.sum(expo, axis=-1)
        accum = accum * rescale[..., None] + jnp.einsum(
            "phqk,pkhd->phqd",
            expo.astype(jnp.bfloat16),
            block_vals,
            preferred_element_type=jnp.float32,
        )
        return ((newest, totals, accum), None)

    carried, unused = lax.scan(advance, carried, blocks)
    maxima, totals, accum = carried
    context = (
        jnp.transpose(accum / totals[..., None], (0, 2, 1, 3))
        .reshape(pages_here, text_len, hq_dec)
        .astype(jnp.bfloat16)
    )
    share = text_len // lax.axis_size("mp")
    mixed = lax.psum_scatter(
        jnp.einsum("pte,ed->tpd", context, wout_dec, preferred_element_type=jnp.float32).astype(
            jnp.bfloat16
        ),
        "mp",
        scatter_dimension=0,
        tiled=True,
    ).astype(jnp.float32)
    own_text = lax.dynamic_slice_in_dim(text_states, lax.axis_index("mp") * share, share, 1)
    decoded = (own_text.astype(jnp.float32) + jnp.moveaxis(mixed, 0, 1)).astype(jnp.bfloat16)
    return (encoded, decoded)


def solution(mesh):
    placed = (
        P(("pages", "batch"), "tile", None, None),
        P(("pages", "batch"), "tile", None),
        P("batch", "mp"),
        P("batch", None, "mp"),
        P("mp", "batch"),
        P("batch", "mp"),
        P("batch", None, "mp"),
        P("mp", "batch"),
    )
    return jax.shard_map(
        body,
        mesh=mesh,
        in_specs=placed,
        out_specs=(
            P(("pages", "batch"), "tile", None, None),
            P(("pages", "batch"), ("tile", "mp"), None),
        ),
        check_vma=False,
    )
```

profile of v0, /device:TPU:0, one launch (start us, length us, event | category | flops | bytes accessed | tf_op | source)
XLA Modules:
  0.0 199.5 jit_solution(16749749369688853707)
XLA Ops:
  7.2 0.7 all-gather.11.cloned.1.call-update
  7.9 0.0 all-gather.9.cloned.1.call-start
  8.0 0.7 all-gather.9.cloned.1.call-update
  8.7 0.7 all-gather.13.cloned.1.call-update
  9.4 0.1 fusion.80
  9.6 5.1 %collective-permute-start = (bf16[1,6,24,1024]{3,2,1,0:T(8,128)(2,1)S(1)}, bf16[1,6,24,1024]{3,2,1,0:T(8,128)(2,1)S(1)}, u32[]{:S(2)}, u32[]{:S(2)}) collective-permute-start(bf16[1,6,24,1024]{3,2,1,0:T(8,128)(2,1)S(1)} %get-tuple-element.29), channel_id=1, source_target_pairs={{0,12},{4,0},{8,4},{12,8},{1,13},{5,1},{9,5},{13,9},{2,14},{6,2},{... | collective-permute-start | bytes 884744 | tf_op jit(solution)/shard_map/ppermute | solution.py:13
  14.7 0.0 all-reduce.2.cloned.1.call-start
  14.8 0.1 add.86
  14.9 0.1 add.82
  14.9 0.1 add.83
  15.0 0.7 broadcast_compare_fusion
  15.8 5.1 %collective-permute-done = bf16[1,6,24,1024]{3,2,1,0:T(8,128)(2,1)S(1)} collective-permute-done((bf16[1,6,24,1024]{3,2,1,0:T(8,128)(2,1)S(1)}, bf16[1,6,24,1024]{3,2,1,0:T(8,128)(2,1)S(1)}, u32[]{:S(2)}, u32[]{:S(2)}) %collective-permute-start) | collective-permute-done | bytes 294944 | tf_op jit(solution)/shard_map/ppermute | solution.py:13
  20.9 0.1 convert_reduce_fusion.1
  21.1 0.3 fusion.31
  21.4 1.5 all-gather.11.cloned.1.call-done
  22.9 2.1 %copy.40 = bf16[128,8,2,512]{3,1,2,0:T(8,128)(2,1)S(1)} copy(bf16[128,8,2,512]{3,2,1,0:T(2,128)(2,1)} %bitcast.102) | data formatting | bytes 4194304
  25.1 9.6 %all-gather.9.cloned.1.call-done = bf16[1024,512]{1,0:T(8,128)(2,1)} async-done(((bf16[512,512]{1,0:T(8,128)(2,1)}), bf16[1024,512]{1,0:T(8,128)(2,1)}) %all-gather.9.cloned.1.call-update) | async-done | bytes 1048592 | tf_op jit(solution)/shard_map/all_gather | solution.py:31
  34.7 2.4 %fusion.12 = bf16[1,12,24,1536]{3,2,1,0:T(8,128)(2,1)S(1)} fusion(bf16[1024,1024]{1,0:T(8,128)(2,1)S(1)} %bitcast.104, bf16[1024,512]{1,0:T(8,128)(2,1)} %all-gather.9.cloned.1.call-done, bf16[6,24,1024]{2,1,0:T(8,128)(2,1)S(1)} %bitcast.106, bf16[6,24,1024]{2,1,0:T(8,128)(2,1)S(1)} %get-tuple-element.28, f32[12,24]{1,0:T(8,128)S(1)} %add_sqrt_fusion.1, ...), kind=kOutput, calls=%fused_computation.17 | convolution fusion | flops 914178048 | bytes 4622592 | tf_op jit(solution)/shard_map/prcd,de->prce/dot_general | solution.py:48
  37.2 0.2 slice.58
  37.4 1.1 pad_maximum_fusion
  38.5 3.7 %reshape.311 = bf16[1,12,2,12,3,16,32]{6,5,4,3,2,1,0:T(8,128)(2,1)S(1)} reshape(bf16[1,12,24,1536]{3,2,1,0:T(8,128)(2,1)} %pad_maximum_fusion) | data formatting | bytes 1769472 | tf_op jit(solution)/shard_map/reshape | solution.py:53
  42.1 0.6 copy.26
  42.8 0.6 fusion.78
  43.4 1.7 copy.39
  45.1 1.0 copy.38
  46.2 1.0 copy.37
  47.2 4.0 %fusion.81 = (f32[2,16,144]{2,1,0:T(8,128)S(1)}, f32[2,16,144,144]{2,3,1,0:T(8,128)}) fusion(pred[2,144,144]{1,2,0:T(8,128)(4,1)S(1)} %copy-done.8, bf16[1,2,144,1,16,32]{2,5,4,1,3,0:T(8,128)(2,1)S(1)} %copy-done.7, bf16[1,2,144,1,16,32]{2,5,4,1,3,0:T(8,128)(2,1)S(1)} %copy.38), kind=kOutput, calls=%fused_computation.103 | convolution fusion | flops 45121680 | bytes 3303936 | tf_op jit(solution)/shard_map/sub | solution.py:75
  51.2 2.8 %fusion.23 = bf16[1,2,144,16,32]{2,4,3,1,0:T(8,128)(2,1)S(1)} fusion(f32[2,16,144,144]{2,3,1,0:T(8,128)} %get-tuple-element.33, f32[2,16,144]{2,1,0:T(8,128)S(1)} %get-tuple-element.32, bf16[1,2,144,1,16,32]{2,5,4,1,3,0:T(8,128)(2,1)S(1)} %copy.37), kind=kOutput, calls=%fused_computation.37 | convolution fusion | flops 43941888 | bytes 3262464 | tf_op jit(solution)/shard_map/pnhqk,pnkhd->pnqhd/dot_general | solution.py:77
  54.0 1.1 copy.31
  55.1 0.9 reshape.316
  56.0 0.1 copy.32
  56.0 0.1 reshape.317
  56.1 0.1 fusion.70
  56.2 1.8 collective-permute-start.1
  58.0 6.2 %collective-permute-done.1 = bf16[1,6,24,512]{3,2,1,0:T(8,128)(2,1)S(1)} collective-permute-done((bf16[1,6,24,512]{3,2,1,0:T(8,128)(2,1)S(1)}, bf16[1,6,24,512]{3,2,1,0:T(8,128)(2,1)S(1)}, u32[]{:S(2)}, u32[]{:S(2)}) %collective-permute-start.1) | collective-permute-done | bytes 147488 | tf_op jit(solution)/shard_map/ppermute | solution.py:13
  64.1 2.5 %fusion.20 = bf16[1,12,24,1024]{3,2,1,0:T(8,128)(2,1)} fusion(bf16[512,1024]{1,0:T(8,128)(2,1)} %all-gather.13.cloned.1.call-done, bf16[1,12,18,512]{3,2,1,0:T(8,128)(2,1)S(1)} %bitcast.99, bf16[1,12,6,512]{3,2,1,0:T(8,128)(2,1)S(1)} %slice.63, bf16[1,6,24,512]{3,2,1,0:T(8,128)(2,1)S(1)} %collective-permute-done.1), kind=kOutput, calls=%fused_computation.34 | convolution fusion | flops 303169536 | bytes 2080768 | tf_op jit(solution)/shard_map/prce,ed->prcd/dot_general | solution.py:85
  66.7 0.0 all-gather.15.cloned.1.call-start
  66.7 0.5 all-gather.15.cloned.1.call-update
  67.3 0.2 all-gather.21.cloned.1.call-start
  67.5 3.6 %copy.41 = bf16[128,8,2,512]{3,1,2,0:T(8,128)(2,1)} copy(bf16[128,8,2,512]{3,2,1,0:T(2,128)(2,1)} %bitcast.101) | data formatting | bytes 4194304
  71.1 25.1 %all-reduce.2.cloned.1.call-done = bf16[1,12,24,1024]{3,2,1,0:T(8,128)(2,1)} async-done(((bf16[1,12,24,1024]{3,2,1,0:T(8,128)(2,1)}), bf16[1,12,24,1024]{3,2,1,0:T(8,128)(2,1)}) %all-reduce.2.cloned.1.call-update) | async-done | bytes 589840 | tf_op jit(solution)/shard_map/psum | solution.py:88
  96.2 1.5 convert_reduce_fusion
  97.7 0.3 fusion.28
  98.0 0.2 fusion.29
  98.3 1.6 convolution_convert_fusion
  99.9 0.0 all-gather.19.cloned.1.call-start
  99.9 0.7 all-gather.19.cloned.1.call-update
  100.6 0.0 reduce-scatter.2.cloned.1.call-start
  100.7 0.1 convert_reduce_fusion.2
  100.8 0.3 fusion.34
  101.1 5.6 %all-gather.15.cloned.1.call-done = bf16[1024,512]{1,0:T(8,128)(2,1)} async-done(((bf16[512,512]{1,0:T(8,128)(2,1)}), bf16[1024,512]{1,0:T(8,128)(2,1)}) %all-gather.15.cloned.1.call-update) | async-done | bytes 1048592 | tf_op jit(solution)/shard_map/all_gather | solution.py:34
  106.8 1.7 convolution_convert_fusion.3
  108.5 0.8 copy.33
  109.3 50.8 %all-gather.21.cloned.1.call-done = bf16[1152,1024]{1,0:T(8,128)(2,1)} async-done(((bf16[288,1024]{1,0:T(8,128)(2,1)}), bf16[1152,1024]{1,0:T(8,128)(2,1)}) %all-gather.21.cloned.1.call-update) | async-done | bytes 2359312 | tf_op jit(solution)/shard_map/all_gather | solution.py:115
  160.1 1.8 fusion.79
  161.9 0.7 copy.34
  162.6 2.5 %multiply_reduce_fusion = (f32[8,256]{1,0:T(8,128)S(1)}, f32[8,256,1152]{2,1,0:T(8,128)S(1)}) fusion(bf16[256,8,64]{0,2,1:T(8,128)(2,1)} %bitcast.108, bf16[1152,8,64]{0,2,1:T(8,128)(2,1)S(1)} %bitcast.97), kind=kOutput, calls=%fused_computation.2 | convolution fusion | flops 306706432 | bytes 10887168 | tf_op jit(solution)/shard_map/while/body/eval_jaxpr/pqhd,pkhd->phqk/dot_general | solution.py:133
  165.1 1.9 fusion.1
  167.0 1.7 copy-done
  168.7 0.7 copy.35
  169.4 5.5 %fusion.40 = bf16[8,256,64]{1,2,0:T(8,128)(2,1)S(1)} fusion(bf16[1152,8,64]{0,2,1:T(8,128)(2,1)S(1)} %bitcast.105, f32[8,256,1152]{2,1,0:T(8,128)} %copy-done, f32[8,256]{1,0:T(8,128)S(1)} %get-tuple-element.34, f32[8,256]{1,0:T(8,128)S(1)} %get-tuple-element.31, f32[8,256]{1,0:T(8,128)S(1)} %get-tuple-element.30), kind=kOutput, calls=%fused_computation.52 | convolution fusion | flops 309460992 | bytes 10903552 | tf_op jit(solution)/shard_map/while/body/eval_jaxpr/phqk,pkhd->phqd/dot_general | solution.py:140
  175.0 2.5 %fusion.24 = bf16[256,1,1024]{2,0,1:T(8,128)(2,1)} fusion(bf16[256,512]{0,1:T(8,128)(2,1)S(1)} %bitcast.110, bf16[512,1024]{1,0:T(8,128)(2,1)} %all-gather.19.cloned.1.call-done), kind=kOutput, calls=%fused_computation.38 | convolution fusion | flops 268697600 | bytes 1835008 | tf_op jit(solution)/shard_map/pte,ed->tpd/dot_general | solution.py:157
  177.6 13.6 %reduce-scatter.2.cloned.1.call-done = bf16[128,1,1024]{2,0,1:T(8,128)(2,1)} async-done(((bf16[256,1,1024]{2,0,1:T(8,128)(2,1)}), bf16[128,1,1024]{2,0,1:T(8,128)(2,1)}) %reduce-scatter.2.cloned.1.call-update) | async-done | bytes 262160 | tf_op jit(solution)/shard_map/reduce_scatter | solution.py:156
  191.2 1.7 fusion.50
  (40 shorter events, 0.4 us)
Async XLA Ops:
  7.2 2.3 %copy-start.4 = (bf16[1,12,24,1024]{3,2,1,0:T(8,128)(2,1)S(1)}, bf16[1,12,24,1024]{3,2,1,0:T(8,128)(2,1)}, u32[]{:S(2)}) copy-start(bf16[1,12,24,1024]{3,2,1,0:T(8,128)(2,1)} %param.8) | copy-start | bytes 1769476
  7.2 15.8 %all-gather.11.cloned.1.call-start = ((), (), s32[]{:S(2)}) async-start(), calls=%async_computation.2 | async-start | bytes 3145728 | tf_op jit(solution)/shard_map/all_gather | solution.py:32
  7.9 26.8 %all-gather.9.cloned.1.call-start = ((), (), s32[]{:S(2)}) async-start(), calls=%async_computation.1 | async-start | bytes 1572864 | tf_op jit(solution)/shard_map/all_gather | solution.py:31
  8.7 49.3 %all-gather.13.cloned.1.call-start = ((), (), s32[]{:S(2)}) async-start(), calls=%async_computation.3 | async-start | bytes 1572864 | tf_op jit(solution)/shard_map/all_gather | solution.py:33
  9.4 58.1 %all-gather.17.cloned.1.call-start = ((), (), s32[]{:S(2)}) async-start(), calls=%async_computation.6 | async-start | bytes 3145728 | tf_op jit(solution)/shard_map/all_gather | solution.py:35
  9.6 11.4 %collective-permute-start = (bf16[1,6,24,1024]{3,2,1,0:T(8,128)(2,1)S(1)}, bf16[1,6,24,1024]{3,2,1,0:T(8,128)(2,1)S(1)}, u32[]{:S(2)}, u32[]{:S(2)}) collective-permute-start(bf16[1,6,24,1024]{3,2,1,0:T(8,128)(2,1)S(1)} %get-tuple-element.29), channel_id=1, source_target_pairs={{0,12},{4,0},{8,4},{12,8},{1,13},{5,1},{9,5},{13,9},{2,14},{6,2},{... | collective-permute-start | bytes 884744 | tf_op jit(solution)/shard_map/ppermute | solution.py:13
  14.7 81.5 %all-reduce.2.cloned.1.call-start = ((), (), s32[]{:S(2)}) async-start(), calls=%async_computation.4 | async-start | bytes 1179648 | tf_op jit(solution)/shard_map/psum | solution.py:88
  45.1 2.1 %copy-start.7 = (bf16[1,2,144,1,16,32]{2,5,4,1,3,0:T(8,128)(2,1)S(1)}, bf16[1,2,144,1,16,32]{2,5,4,1,3,0:T(8,128)(2,1)}, u32[]{:S(2)}) copy-start(bf16[1,2,144,1,16,32]{2,5,4,1,3,0:T(8,128)(2,1)} %copy.39) | copy-start | bytes 884740
  45.1 2.1 %copy-start.8 = (pred[2,144,144]{1,2,0:T(8,128)(4,1)S(1)}, pred[2,144,144]{1,2,0:T(8,128)(4,1)}, u32[]{:S(2)}) copy-start(pred[2,144,144]{1,2,0:T(8,128)(4,1)} %broadcast_compare_fusion) | copy-start | bytes 124420
  56.2 8.0 %collective-permute-start.1 = (bf16[1,6,24,512]{3,2,1,0:T(8,128)(2,1)S(1)}, bf16[1,6,24,512]{3,2,1,0:T(8,128)(2,1)S(1)}, u32[]{:S(2)}, u32[]{:S(2)}) collective-permute-start(bf16[1,6,24,512]{3,2,1,0:T(8,128)(2,1)S(1)} %fusion.70), channel_id=1, source_target_pairs={{0,4},{4,8},{8,12},{12,0},{1,5},{5,9},{9,13},{13,1},{2,6},{6,10},{... | collective-permute-start | bytes 442376 | tf_op jit(solution)/shard_map/ppermute | solution.py:13
  66.7 40.1 %all-gather.15.cloned.1.call-start = ((), (), s32[]{:S(2)}) async-start(), calls=%async_computation.5 | async-start | bytes 1572864 | tf_op jit(solution)/shard_map/all_gather | solution.py:34
  67.3 92.8 %all-gather.21.cloned.1.call-start = ((), (), s32[]{:S(2)}) async-start(), calls=%async_computation.9 | async-start | bytes 2949120 | tf_op jit(solution)/shard_map/all_gather | solution.py:115
  67.5 28.7 %copy-start.5 = (bf16[1,12,24,1024]{3,2,1,0:T(8,128)(2,1)S(1)}, bf16[1,12,24,1024]{3,2,1,0:T(8,128)(2,1)}, u32[]{:S(2)}) copy-start(bf16[1,12,24,1024]{3,2,1,0:T(8,128)(2,1)} %param.8) | copy-start | bytes 1769476
  96.2 2.0 %copy-start.6 = (bf16[128,8,2,512]{3,1,2,0:T(8,128)(2,1)S(1)}, bf16[128,8,2,512]{3,1,2,0:T(8,128)(2,1)}, u32[]{:S(2)}) copy-start(bf16[128,8,2,512]{3,1,2,0:T(8,128)(2,1)} %copy.41) | copy-start | bytes 6291460
  97.7 2.2 %copy-start.1 = (bf16[1,12,24,1024]{3,2,1,0:T(8,128)(2,1)}, bf16[1,12,24,1024]{3,2,1,0:T(8,128)(2,1)S(1)}, u32[]{:S(2)}) copy-start(bf16[1,12,24,1024]{3,2,1,0:T(8,128)(2,1)S(1)} %get-tuple-element.15) | copy-start | bytes 1769476
  98.2 2.4 %copy-start.2 = (bf16[1,256,1024]{2,1,0:T(8,128)(2,1)S(1)}, bf16[1,256,1024]{2,1,0:T(8,128)(2,1)}, u32[]{:S(2)}) copy-start(bf16[1,256,1024]{2,1,0:T(8,128)(2,1)} %param.9) | copy-start | bytes 1572868
  99.9 75.1 %all-gather.19.cloned.1.call-start = ((), (), s32[]{:S(2)}) async-start(), calls=%async_computation.7 | async-start | bytes 1572864 | tf_op jit(solution)/shard_map/all_gather | solution.py:36
  100.6 90.6 %reduce-scatter.2.cloned.1.call-start = ((), (), s32[]{:S(2)}) async-start(), calls=%async_computation.8 | async-start | bytes 786432 | tf_op jit(solution)/shard_map/reduce_scatter | solution.py:156
  165.1 3.7 %copy-start = (f32[8,256,1152]{2,1,0:T(8,128)}, f32[8,256,1152]{2,1,0:T(8,128)S(1)}, u32[]{:S(2)}) copy-start(f32[8,256,1152]{2,1,0:T(8,128)S(1)} %get-tuple-element.35) | copy-start | bytes 28311556
  175.0 16.3 %copy-start.3 = (bf16[1,256,1024]{2,1,0:T(8,128)(2,1)S(1)}, bf16[1,256,1024]{2,1,0:T(8,128)(2,1)}, u32[]{:S(2)}) copy-start(bf16[1,256,1024]{2,1,0:T(8,128)(2,1)} %param.9) | copy-start | bytes 1572868
Sparse Core Ops, SparseCore 0:
  9.6 13.3 all-gather.10
  24.5 10.1 all-gather.8
  36.3 10.1 all-gather.12
  47.9 11.7 all-gather.16
  66.8 29.3 all-reduce.1
  97.7 9.0 all-gather.14
  108.4 51.6 all-gather.20
  161.7 7.8 all-gather.18
  177.7 13.4 reduce-scatter.1
where the time goes:
time: 200 us; the launch traced here: 199 us
  waiting for transfers between devices  121 us (60%)
  matrix products  25.6 us (13%)
  local copies, waits for them, and re-layouts  22.9 us (11%)
  between operations  14.2 us (7%)
  other arithmetic  8.42 us (4%)
  starting transfers between devices  7.43 us (4%)
    all_gather x1, waiting for transfers between devices, body(): shard_rows = lax.all_gather(page_kv, 'tile', axis=1, tiled=True)  50.8 us
    psum x1, waiting for transfers between devices, body(): lax.psum(partial_proj.astype(jnp.bfloat16), 'mp').astype(jnp.float32)  25.1 us
    reduce_scatter x1, waiting for transfers between devices, body(): lax.psum_scatter(jnp.einsum('pte,ed->tpd', context, wout_dec, preferred_e...  13.6 us
    ppermute x2, waiting for transfers between devices, from_behind(): lax.ppermute(value, axis, [(i, (i + by) % devices) for i in range(devices)])  11.3 us
    unnamed x23, local copies, waits for them, and re-layouts  11.3 us
    all_gather x1, waiting for transfers between devices, body(): lax.all_gather(enc_query, 'batch', axis=0, tiled=True)  9.63 us
    ppermute x2, starting transfers between devices, from_behind(): lax.ppermute(value, axis, [(i, (i + by) % devices) for i in range(devices)])  6.9 us
    all_gather x1, waiting for transfers between devices, body(): lax.all_gather(dec_query, 'batch', axis=0, tiled=True)  5.6 us
  transfers between devices with their start and end apart: 11, of which 8 were waited for; matrix products, arithmetic and copies ran while one was open for 25% of the time, Pallas kernels for 0%

commit v1 on v0

--- a/solution.py
+++ b/solution.py
@@ -27,6 +27,16 @@
 
 
 def body(page_cells, text_states, enc_query, enc_keyval, enc_proj, dec_query, dec_keyval, dec_out):
+
+    def launch_the_lines(t0):
+        full_n = lax.axis_size("tile")
+        work_now = [None] * full_n
+        bank = list(map(lambda no: (no, (no + 1) % full_n), range(full_n)))
+        work_now[full_n - 1] = t0
+        for k0 in range(full_n - 2, -1, -1):
+            work_now[k0] = lax.ppermute(work_now[k0 + 1], "tile", bank)
+        return jnp.roll(jnp.concatenate(work_now, 1), (lax.axis_index("tile") + 1) * t0.shape[1], 1)
+
     wq_enc, wkv_enc, wproj_enc, wq_dec, wkv_dec, wout_dec = (
         lax.all_gather(enc_query, "batch", axis=0, tiled=True),
         lax.all_gather(enc_keyval, "batch", axis=0, tiled=True),
@@ -112,7 +122,7 @@
         jnp.zeros((pages_here, heads_dec, text_len, HEAD_DEC), jnp.float32),
     )
     carried = start_state
-    shard_rows = lax.all_gather(page_kv, "tile", axis=1, tiled=True)
+    shard_rows = launch_the_lines(page_kv)
     count = shard_rows.shape[1] // own_rows
     grouped = max(
         (

time: 200 us -> 186 us (0.930)
  waiting for transfers between devices: 121 us -> 104 us
    all_gather x1 -> x0, waiting for transfers between devices: 50.8 us -> none  [body(): shard_rows = lax.all_gather(page_kv, 'tile', axis=1, tiled=True)]
    ppermute x0 -> x3, waiting for transfers between devices: none -> 43.3 us  [launch_the_lines(): work_now[k0] = lax.ppermute(work_now[k0 + 1], 'tile', bank)]
    all_gather x1, waiting for transfers between devices: 5.6 us -> 0.02 us  [body(): lax.all_gather(dec_query, 'batch', axis=0, tiled=True)]
    unnamed x23 -> x24, local copies, waits for them, and re-layouts: 11.3 us -> 11.5 us
  transfers between devices with their start and end apart: 11 -> 13, of which waited for: 8 -> 9; matrix products, arithmetic and copies ran while one was open for 25% -> 28% of each run, Pallas kernels for 0% -> 0%
where the time goes in v1:
time: 186 us
  waiting for transfers between devices  104 us (56%)
  matrix products  25.8 us (14%)
  local copies, waits for them, and re-layouts  23.3 us (13%)
  between operations  14.6 us (8%)
  starting transfers between devices  8.94 us (5%)
  other arithmetic  8.39 us (5%)
    ppermute x3, waiting for transfers between devices, launch_the_lines(): work_now[k0] = lax.ppermute(work_now[k0 + 1], 'tile', bank)  43.3 us
    psum x1, waiting for transfers between devices, body(): lax.psum(partial_proj.astype(jnp.bfloat16), 'mp').astype(jnp.float32)  25.2 us
    reduce_scatter x1, waiting for transfers between devices, body(): lax.psum_scatter(jnp.einsum('pte,ed->tpd', context, wout_dec, preferred_e...  12 us
    unnamed x24, local copies, waits for them, and re-layouts  11.5 us
    ppermute x2, waiting for transfers between devices, from_behind(): lax.ppermute(value, axis, [(i, (i + by) % devices) for i in range(devices)])  11.3 us
    all_gather x1, waiting for transfers between devices, body(): lax.all_gather(enc_query, 'batch', axis=0, tiled=True)  9.63 us
    ppermute x2, starting transfers between devices, from_behind(): lax.ppermute(value, axis, [(i, (i + by) % devices) for i in range(devices)])  6.9 us
    dot_general x1, matrix products, advance(): jnp.einsum('phqk,pkhd->phqd', expo.astype(jnp.bfloat16), block_vals, pref...  5.57 us
  transfers between devices with their start and end apart: 13, of which 9 were waited for; matrix products, arithmetic and copies ran while one was open for 28% of the time, Pallas kernels for 0%

profile of v1, /device:TPU:0, one launch (start us, length us, event | category | flops | bytes accessed | tf_op | source)
XLA Modules:
  0.0 185.5 jit_solution(990386761072446259)
XLA Ops:
  7.2 0.7 all-gather.9.cloned.1.call-update
  7.9 0.0 all-gather.7.cloned.1.call-start
  7.9 0.7 all-gather.7.cloned.1.call-update
  8.7 0.7 all-gather.11.cloned.1.call-update
  9.4 1.2 fusion.80
  10.6 5.1 %collective-permute-start = (bf16[1,6,24,1024]{3,2,1,0:T(8,128)(2,1)S(1)}, bf16[1,6,24,1024]{3,2,1,0:T(8,128)(2,1)S(1)}, u32[]{:S(2)}, u32[]{:S(2)}) collective-permute-start(bf16[1,6,24,1024]{3,2,1,0:T(8,128)(2,1)S(1)} %get-tuple-element.29), channel_id=1, source_target_pairs={{0,12},{4,0},{8,4},{12,8},{1,13},{5,1},{9,5},{13,9},{2,14},{6,2},{... | collective-permute-start | bytes 884744 | tf_op jit(solution)/shard_map/ppermute | solution.py:13
  15.7 0.0 all-reduce.2.cloned.1.call-start
  15.8 0.1 add.99
  15.9 0.1 add.95
  16.0 0.1 add.96
  16.1 0.7 broadcast_compare_fusion
  16.8 5.1 %collective-permute-done = bf16[1,6,24,1024]{3,2,1,0:T(8,128)(2,1)S(1)} collective-permute-done((bf16[1,6,24,1024]{3,2,1,0:T(8,128)(2,1)S(1)}, bf16[1,6,24,1024]{3,2,1,0:T(8,128)(2,1)S(1)}, u32[]{:S(2)}, u32[]{:S(2)}) %collective-permute-start) | collective-permute-done | bytes 294944 | tf_op jit(solution)/shard_map/ppermute | solution.py:13
  22.0 0.1 convert_reduce_fusion.1
  22.1 0.3 fusion.32
  22.4 0.4 all-gather.9.cloned.1.call-done
  22.9 2.1 %copy.40 = bf16[128,8,2,512]{3,1,2,0:T(8,128)(2,1)S(1)} copy(bf16[128,8,2,512]{3,2,1,0:T(2,128)(2,1)} %bitcast.102) | data formatting | bytes 4194304
  25.0 9.6 %all-gather.7.cloned.1.call-done = bf16[1024,512]{1,0:T(8,128)(2,1)} async-done(((bf16[512,512]{1,0:T(8,128)(2,1)}), bf16[1024,512]{1,0:T(8,128)(2,1)}) %all-gather.7.cloned.1.call-update) | async-done | bytes 1048592 | tf_op jit(solution)/shard_map/all_gather | solution.py:41
  34.6 2.4 %fusion.12 = bf16[1,12,24,1536]{3,2,1,0:T(8,128)(2,1)S(1)} fusion(bf16[1024,1024]{1,0:T(8,128)(2,1)S(1)} %bitcast.104, bf16[1024,512]{1,0:T(8,128)(2,1)} %all-gather.7.cloned.1.call-done, bf16[6,24,1024]{2,1,0:T(8,128)(2,1)S(1)} %bitcast.106, bf16[6,24,1024]{2,1,0:T(8,128)(2,1)S(1)} %get-tuple-element.28, f32[12,24]{1,0:T(8,128)S(1)} %add_sqrt_fusion.1, ...), kind=kOutput, calls=%fused_computation.17 | convolution fusion | flops 914178048 | bytes 4622592 | tf_op jit(solution)/shard_map/prcd,de->prce/dot_general | solution.py:58
  37.1 0.2 slice.58
  37.3 1.1 pad_maximum_fusion
  38.4 3.7 %reshape.311 = bf16[1,12,2,12,3,16,32]{6,5,4,3,2,1,0:T(8,128)(2,1)S(1)} reshape(bf16[1,12,24,1536]{3,2,1,0:T(8,128)(2,1)} %pad_maximum_fusion) | data formatting | bytes 1769472 | tf_op jit(solution)/shard_map/reshape | solution.py:63
  42.0 0.6 copy.26
  42.7 0.6 fusion.79
  43.3 1.7 copy.39
  45.0 1.0 copy.38
  46.1 1.0 copy.37
  47.1 5.0 %fusion.81 = (f32[2,16,144]{2,1,0:T(8,128)S(1)}, f32[2,16,144,144]{2,3,1,0:T(8,128)}) fusion(pred[2,144,144]{1,2,0:T(8,128)(4,1)} %broadcast_compare_fusion, bf16[1,2,144,1,16,32]{2,5,4,1,3,0:T(8,128)(2,1)} %copy.39, bf16[1,2,144,1,16,32]{2,5,4,1,3,0:T(8,128)(2,1)S(1)} %copy.38), kind=kOutput, calls=%fused_computation.113 | convolution fusion | flops 45121680 | bytes 3303936 | tf_op jit(solution)/shard_map/sub | solution.py:85
  52.1 2.8 %fusion.24 = bf16[1,2,144,16,32]{2,4,3,1,0:T(8,128)(2,1)S(1)} fusion(f32[2,16,144,144]{2,3,1,0:T(8,128)} %get-tuple-element.33, f32[2,16,144]{2,1,0:T(8,128)S(1)} %get-tuple-element.32, bf16[1,2,144,1,16,32]{2,5,4,1,3,0:T(8,128)(2,1)S(1)} %copy.37), kind=kOutput, calls=%fused_computation.38 | convolution fusion | flops 43941888 | bytes 3262464 | tf_op jit(solution)/shard_map/pnhqk,pnkhd->pnqhd/dot_general | solution.py:87
  54.9 1.1 copy.31
  56.0 0.9 reshape.316
  56.9 0.1 copy.32
  56.9 0.1 reshape.317
  57.0 0.1 fusion.71
  57.1 1.8 collective-permute-start.1
  58.9 6.2 %collective-permute-done.1 = bf16[1,6,24,512]{3,2,1,0:T(8,128)(2,1)S(1)} collective-permute-done((bf16[1,6,24,512]{3,2,1,0:T(8,128)(2,1)S(1)}, bf16[1,6,24,512]{3,2,1,0:T(8,128)(2,1)S(1)}, u32[]{:S(2)}, u32[]{:S(2)}) %collective-permute-start.1) | collective-permute-done | bytes 147488 | tf_op jit(solution)/shard_map/ppermute | solution.py:13
  65.1 2.5 %fusion.20 = bf16[1,12,24,1024]{3,2,1,0:T(8,128)(2,1)} fusion(bf16[512,1024]{1,0:T(8,128)(2,1)} %all-gather.11.cloned.1.call-done, bf16[1,12,18,512]{3,2,1,0:T(8,128)(2,1)S(1)} %bitcast.100, bf16[1,12,6,512]{3,2,1,0:T(8,128)(2,1)S(1)} %slice.63, bf16[1,6,24,512]{3,2,1,0:T(8,128)(2,1)S(1)} %collective-permute-done.1), kind=kOutput, calls=%fused_computation.34 | convolution fusion | flops 303169536 | bytes 2080768 | tf_op jit(solution)/shard_map/prce,ed->prcd/dot_general | solution.py:95
  67.6 0.0 all-gather.13.cloned.1.call-start
  67.7 0.5 all-gather.13.cloned.1.call-update
  68.2 0.2 all-gather.17.cloned.1.call-start
  68.5 3.5 %copy.41 = bf16[128,8,2,512]{3,1,2,0:T(8,128)(2,1)} copy(bf16[128,8,2,512]{3,2,1,0:T(2,128)(2,1)} %bitcast.101) | data formatting | bytes 4194304
  72.0 25.2 %all-reduce.2.cloned.1.call-done = bf16[1,12,24,1024]{3,2,1,0:T(8,128)(2,1)} async-done(((bf16[1,12,24,1024]{3,2,1,0:T(8,128)(2,1)}), bf16[1,12,24,1024]{3,2,1,0:T(8,128)(2,1)}) %all-reduce.2.cloned.1.call-update) | async-done | bytes 589840 | tf_op jit(solution)/shard_map/psum | solution.py:98
  97.1 1.5 convert_reduce_fusion
  98.6 0.3 fusion.29
  98.9 0.2 fusion.30
  99.2 0.8 fusion.21
  100.0 1.5 collective-permute-start.2
  101.5 15.4 %collective-permute-done.2 = bf16[1,288,1024]{2,1,0:T(8,128)(2,1)S(1)} collective-permute-done((bf16[1,288,1024]{2,1,0:T(8,128)(2,1)S(1)}, bf16[1,288,1024]{2,1,0:T(8,128)(2,1)S(1)}, u32[]{:S(2)}, u32[]{:S(2)}) %collective-permute-start.2) | collective-permute-done | bytes 589856 | tf_op jit(solution)/shard_map/ppermute | solution.py:37
  116.9 0.0 reduce-scatter.2.cloned.1.call-start
  117.0 0.1 convert_reduce_fusion.2
  117.1 15.7 %collective-permute-done.3 = bf16[1,288,1024]{2,1,0:T(8,128)(2,1)S(1)} collective-permute-done((bf16[1,288,1024]{2,1,0:T(8,128)(2,1)S(1)}, bf16[1,288,1024]{2,1,0:T(8,128)(2,1)S(1)}, u32[]{:S(2)}, u32[]{:S(2)}) %collective-permute-start.3) | collective-permute-done | bytes 589856 | tf_op jit(solution)/shard_map/ppermute | solution.py:37
  132.9 0.3 fusion.35
  133.2 1.7 convolution_convert_fusion.3
  135.0 0.8 copy.33
  135.8 12.2 %collective-permute-done.4 = bf16[1,288,1024]{2,1,0:T(8,128)(2,1)S(1)} collective-permute-done((bf16[1,288,1024]{2,1,0:T(8,128)(2,1)S(1)}, bf16[1,288,1024]{2,1,0:T(8,128)(2,1)S(1)}, u32[]{:S(2)}, u32[]{:S(2)}) %collective-permute-start.4) | collective-permute-done | bytes 589856 | tf_op jit(solution)/shard_map/ppermute | solution.py:37
  148.3 1.0 constant_dynamic-slice_fusion
  149.3 0.7 copy.34
  150.0 2.5 %multiply_reduce_fusion = (f32[8,256]{1,0:T(8,128)S(1)}, f32[8,256,1152]{2,1,0:T(8,128)S(1)}) fusion(bf16[256,8,64]{0,2,1:T(8,128)(2,1)} %bitcast.108, bf16[1152,8,64]{0,2,1:T(8,128)(2,1)S(1)} %bitcast.98), kind=kOutput, calls=%fused_computation.2 | convolution fusion | flops 306706432 | bytes 10887168 | tf_op jit(solution)/shard_map/while/body/eval_jaxpr/pqhd,pkhd->phqk/dot_general | solution.py:143
  152.5 1.9 %fusion.1 = f32[8,256]{1,0:T(8,128)S(1)} fusion(f32[8,256,1152]{2,1,0:T(8,128)S(1)} %get-tuple-element.35, f32[8,256]{1,0:T(8,128)S(1)} %get-tuple-element.34), kind=kLoop, calls=%fused_computation.3 | loop fusion | flops 7075840 | bytes 9453568 | tf_op jit(solution)/shard_map/while/body/eval_jaxpr/reduce_sum | solution.py:149
  154.4 1.7 copy-done
  156.1 0.7 copy.35
  156.9 5.6 %fusion.41 = bf16[8,256,64]{1,2,0:T(8,128)(2,1)S(1)} fusion(bf16[1152,8,64]{0,2,1:T(8,128)(2,1)S(1)} %bitcast.105, f32[8,256,1152]{2,1,0:T(8,128)} %copy-done, f32[8,256]{1,0:T(8,128)S(1)} %get-tuple-element.34, f32[8,256]{1,0:T(8,128)S(1)} %get-tuple-element.31, f32[8,256]{1,0:T(8,128)S(1)} %get-tuple-element.30), kind=kOutput, calls=%fused_computation.53 | convolution fusion | flops 309460992 | bytes 10903552 | tf_op jit(solution)/shard_map/while/body/eval_jaxpr/phqk,pkhd->phqd/dot_general | solution.py:150
  162.5 2.5 %fusion.25 = bf16[256,1,1024]{2,0,1:T(8,128)(2,1)} fusion(bf16[256,512]{0,1:T(8,128)(2,1)S(1)} %bitcast.110, bf16[512,1024]{1,0:T(8,128)(2,1)} %all-gather.17.cloned.1.call-done), kind=kOutput, calls=%fused_computation.39 | convolution fusion | flops 268697600 | bytes 1835008 | tf_op jit(solution)/shard_map/pte,ed->tpd/dot_general | solution.py:167
  165.0 12.0 %reduce-scatter.2.cloned.1.call-done = bf16[128,1,1024]{2,0,1:T(8,128)(2,1)} async-done(((bf16[256,1,1024]{2,0,1:T(8,128)(2,1)}), bf16[128,1,1024]{2,0,1:T(8,128)(2,1)}) %reduce-scatter.2.cloned.1.call-update) | async-done | bytes 262160 | tf_op jit(solution)/shard_map/reduce_scatter | solution.py:166
  177.0 1.7 fusion.51
  (45 shorter events, 0.7 us)
Async XLA Ops:
  7.2 15.7 %all-gather.9.cloned.1.call-start = ((), (), s32[]{:S(2)}) async-start(), calls=%async_computation.2 | async-start | bytes 3145728 | tf_op jit(solution)/shard_map/all_gather | solution.py:42
  7.9 26.7 %all-gather.7.cloned.1.call-start = ((), (), s32[]{:S(2)}) async-start(), calls=%async_computation.1 | async-start | bytes 1572864 | tf_op jit(solution)/shard_map/all_gather | solution.py:41
  8.6 50.3 %all-gather.11.cloned.1.call-start = ((), (), s32[]{:S(2)}) async-start(), calls=%async_computation.3 | async-start | bytes 1572864 | tf_op jit(solution)/shard_map/all_gather | solution.py:43
  9.4 59.1 %all-gather.15.cloned.1.call-start = ((), (), s32[]{:S(2)}) async-start(), calls=%async_computation.6 | async-start | bytes 3145728 | tf_op jit(solution)/shard_map/all_gather | solution.py:45
  10.6 11.4 %collective-permute-start = (bf16[1,6,24,1024]{3,2,1,0:T(8,128)(2,1)S(1)}, bf16[1,6,24,1024]{3,2,1,0:T(8,128)(2,1)S(1)}, u32[]{:S(2)}, u32[]{:S(2)}) collective-permute-start(bf16[1,6,24,1024]{3,2,1,0:T(8,128)(2,1)S(1)} %get-tuple-element.29), channel_id=1, source_target_pairs={{0,12},{4,0},{8,4},{12,8},{1,13},{5,1},{9,5},{13,9},{2,14},{6,2},{... | collective-permute-start | bytes 884744 | tf_op jit(solution)/shard_map/ppermute | solution.py:13
  15.7 81.4 %all-reduce.2.cloned.1.call-start = ((), (), s32[]{:S(2)}) async-start(), calls=%async_computation.4 | async-start | bytes 1179648 | tf_op jit(solution)/shard_map/psum | solution.py:98
  57.1 40.0 %copy-start.4 = (bf16[1,12,24,1024]{3,2,1,0:T(8,128)(2,1)S(1)}, bf16[1,12,24,1024]{3,2,1,0:T(8,128)(2,1)}, u32[]{:S(2)}) copy-start(bf16[1,12,24,1024]{3,2,1,0:T(8,128)(2,1)} %param.8) | copy-start | bytes 1769476
  57.1 8.0 %collective-permute-start.1 = (bf16[1,6,24,512]{3,2,1,0:T(8,128)(2,1)S(1)}, bf16[1,6,24,512]{3,2,1,0:T(8,128)(2,1)S(1)}, u32[]{:S(2)}, u32[]{:S(2)}) collective-permute-start(bf16[1,6,24,512]{3,2,1,0:T(8,128)(2,1)S(1)} %fusion.71), channel_id=1, source_target_pairs={{0,4},{4,8},{8,12},{12,0},{1,5},{5,9},{9,13},{13,1},{2,6},{6,10},{... | collective-permute-start | bytes 442376 | tf_op jit(solution)/shard_map/ppermute | solution.py:13
  67.6 65.6 %all-gather.13.cloned.1.call-start = ((), (), s32[]{:S(2)}) async-start(), calls=%async_computation.5 | async-start | bytes 1572864 | tf_op jit(solution)/shard_map/all_gather | solution.py:44
  68.2 94.3 %all-gather.17.cloned.1.call-start = ((), (), s32[]{:S(2)}) async-start(), calls=%async_computation.7 | async-start | bytes 1572864 | tf_op jit(solution)/shard_map/all_gather | solution.py:46
  97.1 2.0 %copy-start.5 = (bf16[128,8,2,512]{3,1,2,0:T(8,128)(2,1)S(1)}, bf16[128,8,2,512]{3,1,2,0:T(8,128)(2,1)}, u32[]{:S(2)}) copy-start(bf16[128,8,2,512]{3,1,2,0:T(8,128)(2,1)} %copy.41) | copy-start | bytes 6291460
  98.6 18.3 %copy-start.1 = (bf16[1,12,24,1024]{3,2,1,0:T(8,128)(2,1)}, bf16[1,12,24,1024]{3,2,1,0:T(8,128)(2,1)S(1)}, u32[]{:S(2)}) copy-start(bf16[1,12,24,1024]{3,2,1,0:T(8,128)(2,1)S(1)} %get-tuple-element.15) | copy-start | bytes 1769476
  98.9 18.1 %copy-start.2 = (bf16[1,256,1024]{2,1,0:T(8,128)(2,1)S(1)}, bf16[1,256,1024]{2,1,0:T(8,128)(2,1)}, u32[]{:S(2)}) copy-start(bf16[1,256,1024]{2,1,0:T(8,128)(2,1)} %param.9) | copy-start | bytes 1572868
  100.0 16.9 %collective-permute-start.2 = (bf16[1,288,1024]{2,1,0:T(8,128)(2,1)S(1)}, bf16[1,288,1024]{2,1,0:T(8,128)(2,1)S(1)}, u32[]{:S(2)}, u32[]{:S(2)}) collective-permute-start(bf16[1,288,1024]{2,1,0:T(8,128)(2,1)S(1)} %fusion.21), channel_id=1, source_target_pairs={{0,4},{4,8},{8,12},{12,0},{1,5},{5,9},{9,13},{13,1},{2,6},{6,10},{... | collective-permute-start | bytes 1769480 | tf_op jit(solution)/shard_map/ppermute | solution.py:37
  116.9 16.0 %collective-permute-start.3 = (bf16[1,288,1024]{2,1,0:T(8,128)(2,1)S(1)}, bf16[1,288,1024]{2,1,0:T(8,128)(2,1)S(1)}, u32[]{:S(2)}, u32[]{:S(2)}) collective-permute-start(bf16[1,288,1024]{2,1,0:T(8,128)(2,1)S(1)} %collective-permute-done.2), channel_id=1, source_target_pairs={{0,4},{4,8},{8,12},{12,0},{1,5},{5,9},{9,13},{13,1},{2,6},{6,10},{... | collective-permute-start | bytes 1769480 | tf_op jit(solution)/shard_map/ppermute | solution.py:37
  116.9 60.0 %reduce-scatter.2.cloned.1.call-start = ((), (), s32[]{:S(2)}) async-start(), calls=%async_computation.8 | async-start | bytes 786432 | tf_op jit(solution)/shard_map/reduce_scatter | solution.py:166
  132.9 15.1 %collective-permute-start.4 = (bf16[1,288,1024]{2,1,0:T(8,128)(2,1)S(1)}, bf16[1,288,1024]{2,1,0:T(8,128)(2,1)S(1)}, u32[]{:S(2)}, u32[]{:S(2)}) collective-permute-start(bf16[1,288,1024]{2,1,0:T(8,128)(2,1)S(1)} %collective-permute-done.3), channel_id=1, source_target_pairs={{0,4},{4,8},{8,12},{12,0},{1,5},{5,9},{9,13},{13,1},{2,6},{6,10},{... | collective-permute-start | bytes 1769480 | tf_op jit(solution)/shard_map/ppermute | solution.py:37
  152.5 3.6 %copy-start = (f32[8,256,1152]{2,1,0:T(8,128)}, f32[8,256,1152]{2,1,0:T(8,128)S(1)}, u32[]{:S(2)}) copy-start(f32[8,256,1152]{2,1,0:T(8,128)S(1)} %get-tuple-element.35) | copy-start | bytes 28311556
  156.9 20.1 %copy-start.3 = (bf16[1,256,1024]{2,1,0:T(8,128)(2,1)S(1)}, bf16[1,256,1024]{2,1,0:T(8,128)(2,1)}, u32[]{:S(2)}) copy-start(bf16[1,256,1024]{2,1,0:T(8,128)(2,1)} %param.9) | copy-start | bytes 1572868
Sparse Core Ops, SparseCore 0:
  9.5 13.2 all-gather.8
  24.4 10.1 all-gather.6
  36.2 10.1 all-gather.10
  47.8 11.7 all-gather.14
  67.7 29.3 all-reduce.1
  98.6 9.0 all-gather.12
  117.0 9.5 all-gather.16
  165.1 11.7 reduce-scatter.1
